TPU v7x, 32 devices: a whole 2x2x4 slice. The times are simulated.
32 devices in a mesh: dp: 8 (over y, x, core), own: 4 (over z).
Axes of the slice: x: 2, y: 2, z: 4, core: 2. Of those that a mesh axis runs over, the one named last changes fastest.
Arguments:
- grads: bfloat16 [8, 6, 8192, 128], P('dp', None, 'own'), may hold values from -6 to 6
- proj: bfloat16 [4, 3, 8192, 1024], P('own', None, 'dp'), may hold values from -0.0625 to 0.0625
- moment1: float32 [4, 3, 1024, 128], P('own', None, 'dp'), may hold values from -24 to 24
- moment2: float32 [4, 3, 1024, 128], P('own', None, 'dp'), may hold values from 0.05 to 5
- plan: int32 [6], replicated, may hold values from 0 to 3, as said below
Outputs:
- update: bfloat16 [6, 8192, 128], P(None, 'own')
- new_moment1: float32 [4, 3, 1024, 128], P('own', None, 'dp')
- new_moment2: float32 [4, 3, 1024, 128], P('own', None, 'dp')
Inputs may be any that keep to these rules, and one draw needn't show every extreme that they name: `plan`: no owner is named more than 3 times, and some owner is named exactly 3 times.
All inputs are finite; a program needn't handle non-finite values.
Results may differ from a plain program's by a relative error of at most 0.015.
Values may be sent and summed in bfloat16 or wider, within the bound.
A program may use at most 64 MiB of HBM per device.

v0:
```python
import jax
import jax.numpy as jnp
from jax import lax
from jax.sharding import PartitionSpec as P

beta_one = 0.9
beta_two = 0.999
adam_eps = 1e-08
norm_eps = 1e-06
correct_one = 1.0 - 0.9**10
correct_two = 1.0 - 0.999**10


def slot_selector(plan, owner_count, capacity):
    matrices = plan.shape[0]
    places = jnp.arange(owner_count * capacity, dtype=jnp.int32)
    owners = places // capacity
    within = places % capacity
    index = jnp.arange(matrices, dtype=jnp.int32)
    before = jnp.sum(
        ((plan[None, :] == plan[:, None]) & (index[None, :] < index[:, None])).astype(jnp.int32),
        axis=1,
    )
    chosen = (plan[None, :] == owners[:, None]) & (before[None, :] == within[:, None])
    return chosen.astype(jnp.bfloat16)


def adam_moments(rank_share, first_old, second_old):
    first_new = beta_one * first_old + (1.0 - beta_one) * rank_share
    second_new = beta_two * second_old + (1.0 - beta_two) * rank_share * rank_share
    adam_step = first_new / correct_one / (jnp.sqrt(second_new / correct_two) + adam_eps)
    return (first_new, second_new, adam_step.astype(jnp.bfloat16))


def local(grads, proj, moment1, moment2, plan):
    owner_count = lax.axis_size("own")
    replica_count = lax.axis_size("dp")
    capacity = proj.shape[1]
    own_rows = grads.shape[2]
    columns = grads.shape[3]
    rank_rows = moment1.shape[2]
    selector = slot_selector(plan, owner_count, capacity)
    outgoing = jnp.einsum(
        "sj,jdc->sdc", selector, grads[0], preferred_element_type=jnp.float32
    ).astype(jnp.bfloat16)
    group_ratio = replica_count // owner_count
    piece_rows = own_rows // replica_count
    blocked = outgoing.reshape(owner_count * capacity, replica_count, piece_rows, columns)
    pieces = lax.psum_scatter(blocked, "dp", scatter_dimension=1, tiled=True).astype(jnp.float32)
    pieces = pieces.reshape(owner_count, capacity, piece_rows, columns)
    routed = lax.all_to_all(
        pieces.astype(jnp.bfloat16), "own", split_axis=0, concat_axis=0, tiled=True
    ).astype(pieces.dtype)
    span_pos = lax.axis_index("dp") // owner_count
    marker = (jnp.arange(group_ratio, dtype=jnp.int32) == span_pos).astype(jnp.float32)
    placed = routed[:, None] * marker[None, :, None, None, None]
    placed = placed.reshape(replica_count, capacity, piece_rows, columns)
    received = lax.all_to_all(
        placed.astype(jnp.bfloat16), "dp", split_axis=0, concat_axis=0, tiled=True
    ).astype(placed.dtype)
    received = received.reshape(group_ratio, owner_count, capacity, piece_rows, columns)
    mine = lax.axis_index("dp") % group_ratio
    kept = lax.dynamic_index_in_dim(received, mine, 0, keepdims=False)
    summed = jnp.transpose(kept, (1, 0, 2, 3)).reshape(capacity, owner_count * piece_rows, columns)
    grad_half = summed.astype(jnp.bfloat16)
    projection = proj[0]
    partial_value = jnp.einsum(
        "kdr,kdc->krc", projection, grad_half, preferred_element_type=jnp.float32
    )
    first_old = moment1[0]
    second_old = moment2[0]
    rank_full = lax.psum(partial_value.astype(jnp.bfloat16), "dp").astype(jnp.float32)
    rank_start = lax.axis_index("dp") * rank_rows
    rank_share = lax.dynamic_slice_in_dim(rank_full, rank_start, rank_rows, 1)
    first_new, second_new, adam_half = adam_moments(rank_share, first_old, second_old)
    adam_full = lax.all_gather(adam_half, "dp", axis=1, tiled=True)
    rank_half = rank_full.astype(jnp.bfloat16)
    grad_norms = jnp.sum(rank_full * rank_full, axis=1)
    adam_wide = adam_full.astype(jnp.float32)
    step_norms = jnp.sum(adam_wide * adam_wide, axis=1)
    column_scale = jnp.sqrt(step_norms) / (jnp.sqrt(grad_norms) + norm_eps)
    combined = (adam_wide - column_scale[:, None, :] * rank_half.astype(jnp.float32)).astype(
        jnp.bfloat16
    )
    update_full = (
        jnp.einsum("kdr,krc->kdc", projection, combined, preferred_element_type=jnp.float32)
        + column_scale[:, None, :] * summed
    )
    update_half = update_full.astype(jnp.bfloat16)
    gathered = lax.all_gather(update_half, "dp", axis=1, tiled=True)
    gathered = gathered.reshape(capacity, owner_count, own_rows, columns)
    returned = lax.all_to_all(gathered, "own", split_axis=1, concat_axis=0, tiled=True)
    slot_rows = returned.reshape(owner_count * capacity, own_rows, columns)
    update = jnp.einsum(
        "sj,sdc->jdc", selector, slot_rows, preferred_element_type=jnp.float32
    ).astype(jnp.bfloat16)
    return (update, first_new[None], second_new[None])


def solution(mesh):
    return jax.shard_map(
        local,
        mesh=mesh,
        in_specs=(
            P("dp", None, "own", None),
            P("own", None, "dp", None),
            P("own", None, "dp", None),
            P("own", None, "dp", None),
            P(),
        ),
        out_specs=(P(None, "own", None), P("own", None, "dp", None), P("own", None, "dp", None)),
        check_vma=False,
    )
```

profile of v0, /device:TPU:0, one launch (start us, length us, event | category | flops | bytes accessed | tf_op | source)
XLA Modules:
  0.0 447.2 jit_solution(17571062850924733432)
XLA Ops:
  7.2 0.0 copy-start
  7.2 0.0 reduce-scatter.2.cloned.1.call-start
  7.2 1.0 convert_reduce_fusion
  8.2 0.8 copy-done
  9.1 13.2 %convolution_convert_fusion = bf16[12,2048,128]{2,0,1:T(8,128)(2,1)S(1)} fusion(bf16[6,2048,128]{2,1,0:T(8,128)(2,1)S(1)} %bitcast.60, s32[12]{0:T(128)S(1)} %get-tuple-element.18, s32[12]{0:T(128)S(1)} %get-tuple-element.19, s32[6]{0:T(128)S(1)} %convert_reduce_fusion, s32[6]{0:T(128)} %param.9), kind=kOutput, calls=%fused_computation.2 | convolution fusion | flops 40894680 | bytes 9437328 | tf_op jit(solution)/shard_map/sj,jdc->sdc/dot_general | solution.py:43
  22.3 4.4 copy.37
  26.8 0.0 reduce-scatter.2.cloned.1.call-update
  26.8 64.6 %reduce-scatter.2.cloned.1.call-done = bf16[12,1,256,128]{3,2,0,1:T(8,128)(2,1)} async-done(((bf16[12,8,256,128]{3,2,0,1:T(8,128)(2,1)}), bf16[12,1,256,128]{3,2,0,1:T(8,128)(2,1)}) %reduce-scatter.2.cloned.1.call-update) | async-done | bytes 786448 | tf_op jit(solution)/shard_map/reduce_scatter | solution.py:49
  91.4 4.6 %all-to-all-start = ((bf16[4,3,256,128]{3,2,1,0:T(8,128)(2,1)}), bf16[4,3,256,128]{3,2,1,0:T(8,128)(2,1)S(1)}, u32[]{:S(2)}, u32[]{:S(2)}) async-start(bf16[4,3,256,128]{3,2,1,0:T(8,128)(2,1)} %bitcast.63), calls=%async_computation.1 | async-start | bytes 1572864 | tf_op jit(solution)/shard_map/all_to_all | solution.py:51
  96.0 0.1 mul.82
  96.1 19.8 %all-to-all-done = bf16[4,3,256,128]{3,2,1,0:T(8,128)(2,1)S(1)} async-done(((bf16[4,3,256,128]{3,2,1,0:T(8,128)(2,1)}), bf16[4,3,256,128]{3,2,1,0:T(8,128)(2,1)S(1)}, u32[]{:S(2)}, u32[]{:S(2)}) %all-to-all-start) | async-done | bytes 786464 | tf_op jit(solution)/shard_map/all_to_all | solution.py:51
  116.0 0.1 convert_element_type.58
  116.1 1.6 fusion.7
  117.7 3.6 all-to-all-start.1
  121.3 0.0 all-reduce.2.cloned.1.call-start
  121.3 20.9 %all-to-all-done.1 = bf16[8,3,256,128]{3,2,1,0:T(8,128)(2,1)S(1)} async-done(((bf16[8,3,256,128]{3,2,1,0:T(8,128)(2,1)}), bf16[8,3,256,128]{3,2,1,0:T(8,128)(2,1)S(1)}, u32[]{:S(2)}, u32[]{:S(2)}) %all-to-all-start.1) | async-done | bytes 1572896 | tf_op jit(solution)/shard_map/all_to_all | solution.py:58
  142.2 0.1 convert_bitcast_fusion
  142.4 0.8 copy.38
  143.2 0.8 reshape.73
  144.0 0.0 copy-start.3
  144.0 0.0 copy-start.4
  144.0 4.7 %fusion.19 = bf16[3,1024,128]{1,2,0:T(8,128)(2,1)} fusion(bf16[1,3,1024,1024]{3,2,1,0:T(8,128)(2,1)} %param.6, f32[3,1024,128]{1,2,0:T(8,128)S(1)} %reshape.73), kind=kOutput, calls=%fused_computation.20 | convolution fusion | flops 806092800 | bytes 8650752 | tf_op jit(solution)/shard_map/kdr,kdc->krc/dot_general | solution.py:67
  148.8 0.0 all-reduce.2.cloned.1.call-update
  148.8 0.0 all-gather.2.cloned.1.call-start
  148.8 0.0 copy-done.3
  148.8 0.1 copy.35
  149.0 0.0 copy-done.4
  149.0 0.1 copy.39
  149.1 52.7 %all-reduce.2.cloned.1.call-done = bf16[3,1024,128]{1,2,0:T(8,128)(2,1)} async-done(((bf16[3,1024,128]{1,2,0:T(8,128)(2,1)}), bf16[3,1024,128]{1,2,0:T(8,128)(2,1)}) %all-reduce.2.cloned.1.call-update) | async-done | bytes 786448 | tf_op jit(solution)/shard_map/psum | solution.py:72
  201.8 1.4 convert_element_type.64
  203.2 0.2 fusion.28
  203.4 10.0 %all_gather.6 = bf16[3,1024,128]{1,2,0:T(8,128)(2,1)S(1)} all-gather(bf16[3,128,128]{1,2,0:T(8,128)(2,1)S(1)} %get-tuple-element.16), channel_id=1, replica_groups=mesh['dp'=8,'own'=4] {'dp'}, dimensions={1}, use_global_device_ids=true | all-gather | bytes 884736 | tf_op jit(solution)/shard_map/all_gather | solution.py:76
  213.4 0.2 fusion.11
  213.6 0.0 copy-done.2
  213.6 0.2 multiply_reduce_fusion
  213.9 5.9 %fusion.13 = bf16[3,1024,128]{1,2,0:T(8,128)(2,1)} fusion(f32[3,1024,128]{1,2,0:T(8,128)S(1)} %reshape.73, bf16[1,3,1024,1024]{3,2,1,0:T(8,128)(2,1)} %param.6, bf16[3,1024,128]{1,2,0:T(8,128)(2,1)S(1)} %all_gather.6, f32[3,128]{1,0:T(4,128)S(1)} %add_divide_fusion, bf16[3,1024,128]{1,2,0:T(8,128)(2,1)S(1)} %copy-done.2), kind=kOutput, calls=%fused_computation.17 | convolution fusion | flops 808452096 | bytes 10225152 | tf_op jit(solution)/shard_map/kdr,krc->kdc/dot_general | solution.py:86
  219.8 0.0 all-gather.2.cloned.1.call-update
  219.8 45.6 %all-gather.2.cloned.1.call-done = bf16[3,8192,128]{1,2,0:T(8,128)(2,1)} async-done(((bf16[3,1024,128]{1,2,0:T(8,128)(2,1)}), bf16[3,8192,128]{1,2,0:T(8,128)(2,1)}) %all-gather.2.cloned.1.call-update) | async-done | bytes 6291472 | tf_op jit(solution)/shard_map/all_gather | solution.py:90
  265.4 11.1 %reshape.74 = bf16[3,4,2048,128]{2,1,3,0:T(4,128)(2,1)} reshape(bf16[3,8192,128]{1,2,0:T(8,128)(2,1)} %all-gather.2.cloned.1.call-done) | data formatting | bytes 12582912 | tf_op jit(solution)/shard_map/reshape | solution.py:91
  276.5 11.2 %copy.40 = bf16[3,4,2048,128]{3,2,0,1:T(8,128)(2,1)} copy(bf16[3,4,2048,128]{2,1,3,0:T(4,128)(2,1)} %reshape.74) | data formatting | bytes 12582912 | tf_op jit(solution)/shard_map/reshape | solution.py:91
  287.7 5.4 %all-to-all-start.2 = ((bf16[3,4,2048,128]{3,2,0,1:T(8,128)(2,1)}), bf16[3,4,2048,128]{3,2,0,1:T(8,128)(2,1)}, u32[]{:S(2)}, u32[]{:S(2)}) async-start(bf16[3,4,2048,128]{3,2,0,1:T(8,128)(2,1)} %copy.40), calls=%async_computation.3 | async-start | bytes 12582912 | tf_op jit(solution)/shard_map/all_to_all | solution.py:92
  293.1 0.8 copy.43
  293.9 0.8 copy.44
  294.7 137.2 %all-to-all-done.2 = bf16[3,4,2048,128]{3,2,0,1:T(8,128)(2,1)} async-done(((bf16[3,4,2048,128]{3,2,0,1:T(8,128)(2,1)}), bf16[3,4,2048,128]{3,2,0,1:T(8,128)(2,1)}, u32[]{:S(2)}, u32[]{:S(2)}) %all-to-all-start.2) | async-done | bytes 6291488 | tf_op jit(solution)/shard_map/all_to_all | solution.py:92
  431.9 0.0 copy-done.5
  431.9 6.7 %fusion.8 = bf16[6,2048,128]{2,0,1:T(8,128)(2,1)S(1)} fusion(bf16[12,2048,128]{2,1,0:T(8,128)(2,1)} %bitcast.15, s32[12]{0:T(128)S(1)} %get-tuple-element.18, s32[12]{0:T(128)S(1)} %get-tuple-element.19, s32[6]{0:T(128)S(1)} %convert_reduce_fusion, s32[6]{0:T(128)S(1)} %copy-done.5), kind=kOutput, calls=%fused_computation.10 | convolution fusion | flops 39321816 | bytes 9437328 | tf_op jit(solution)/shard_map/sj,sdc->jdc/dot_general | solution.py:94
  438.6 2.1 copy.42
  440.7 0.0 copy-done.1
  (7 shorter events, 0.0 us)
Async XLA Ops:
  7.2 1.9 copy-start
  7.2 84.2 %reduce-scatter.2.cloned.1.call-start = ((), (), s32[]{:S(2)}) async-start(), calls=%async_computation.4 | async-start | bytes 7077888 | tf_op jit(solution)/shard_map/reduce_scatter | solution.py:49
  91.4 24.6 %all-to-all-start = ((bf16[4,3,256,128]{3,2,1,0:T(8,128)(2,1)}), bf16[4,3,256,128]{3,2,1,0:T(8,128)(2,1)S(1)}, u32[]{:S(2)}, u32[]{:S(2)}) async-start(bf16[4,3,256,128]{3,2,1,0:T(8,128)(2,1)} %bitcast.63), calls=%async_computation.1 | async-start | bytes 1572864 | tf_op jit(solution)/shard_map/all_to_all | solution.py:51
  117.7 24.5 %all-to-all-start.1 = ((bf16[8,3,256,128]{3,2,1,0:T(8,128)(2,1)}), bf16[8,3,256,128]{3,2,1,0:T(8,128)(2,1)S(1)}, u32[]{:S(2)}, u32[]{:S(2)}) async-start(bf16[8,3,256,128]{3,2,1,0:T(8,128)(2,1)} %fusion.7), calls=%async_computation.2 | async-start | bytes 3145728 | tf_op jit(solution)/shard_map/all_to_all | solution.py:58
  121.3 80.5 %all-reduce.2.cloned.1.call-start = ((), (), s32[]{:S(2)}) async-start(), calls=%async_computation.5 | async-start | bytes 1572864 | tf_op jit(solution)/shard_map/psum | solution.py:72
  144.0 4.8 %copy-start.3 = (f32[1,3,128,128]{3,2,1,0:T(8,128)S(1)}, f32[1,3,128,128]{3,2,1,0:T(8,128)}, u32[]{:S(2)}) copy-start(f32[1,3,128,128]{3,2,1,0:T(8,128)} %param.7) | copy-start | bytes 589828
  144.0 4.9 %copy-start.4 = (f32[1,3,128,128]{3,2,1,0:T(8,128)S(1)}, f32[1,3,128,128]{3,2,1,0:T(8,128)}, u32[]{:S(2)}) copy-start(f32[1,3,128,128]{3,2,1,0:T(8,128)} %param.8) | copy-start | bytes 589828
  148.8 116.6 %all-gather.2.cloned.1.call-start = ((), (), s32[]{:S(2)}) async-start(), calls=%async_computation.6 | async-start | bytes 7077888 | tf_op jit(solution)/shard_map/all_gather | solution.py:90
  201.8 11.8 %copy-start.2 = (bf16[3,1024,128]{1,2,0:T(8,128)(2,1)S(1)}, bf16[3,1024,128]{1,2,0:T(8,128)(2,1)}, u32[]{:S(2)}) copy-start(bf16[3,1024,128]{1,2,0:T(8,128)(2,1)} %all-reduce.2.cloned.1.call-done) | copy-start | bytes 2359300
  287.7 144.2 %copy-start.5 = (s32[6]{0:T(128)S(1)}, s32[6]{0:T(128)}, u32[]{:S(2)}) copy-start(s32[6]{0:T(128)} %param.9) | copy-start | bytes 76
  287.7 144.2 %all-to-all-start.2 = ((bf16[3,4,2048,128]{3,2,0,1:T(8,128)(2,1)}), bf16[3,4,2048,128]{3,2,0,1:T(8,128)(2,1)}, u32[]{:S(2)}, u32[]{:S(2)}) async-start(bf16[3,4,2048,128]{3,2,0,1:T(8,128)(2,1)} %copy.40), calls=%async_computation.3 | async-start | bytes 12582912 | tf_op jit(solution)/shard_map/all_to_all | solution.py:92
  431.9 8.7 %copy-start.1 = (bf16[1,6,2048,128]{3,2,1,0:T(8,128)(2,1)S(1)}, bf16[1,6,2048,128]{3,2,1,0:T(8,128)(2,1)}, u32[]{:S(2)}) copy-start(bf16[1,6,2048,128]{3,2,1,0:T(8,128)(2,1)} %param.5) | copy-start | bytes 9437188
Sparse Core Ops, SparseCore 0:
  26.9 64.4 reduce-scatter.1
  148.9 52.8 all-reduce.1
  219.9 45.3 all-gather.1
where the time goes:
time: 448 us; the launch traced here: 447 us
  waiting for transfers between devices  341 us (76%)
  local copies, waits for them, and re-layouts  33.4 us (7%)
  matrix products  30.5 us (7%)
  between operations  13.9 us (3%)
  starting transfers between devices  13.7 us (3%)
  blocking collectives  10 us (2%)
  other arithmetic  4.87 us (1%)
    all_to_all x1, waiting for transfers between devices, local(): lax.all_to_all(gathered, 'own', split_axis=1, concat_axis=0, tiled=True)  137 us
    reduce_scatter x1, waiting for transfers between devices, local(): lax.psum_scatter(blocked, 'dp', scatter_dimension=1, tiled=True)  64.6 us
    psum x1, waiting for transfers between devices, local(): lax.psum(partial_value.astype(jnp.bfloat16), 'dp').astype(jnp.float32)  52.7 us
    all_gather x1, waiting for transfers between devices, local(): gathered = lax.all_gather(update_half, 'dp', axis=1, tiled=True)  45.6 us
    reshape x2, local copies, waits for them, and re-layouts, local(): gathered = gathered.reshape(capacity, owner_count, own_rows, columns)  22.4 us
    all_to_all x1, waiting for transfers between devices, local(): lax.all_to_all(placed.astype(jnp.bfloat16), 'dp', split_axis=0, concat_ax...  20.9 us
    all_to_all x1, waiting for transfers between devices, local(): lax.all_to_all(pieces.astype(jnp.bfloat16), 'own', split_axis=0, concat_a...  19.8 us
    dot_general x1, matrix products, local(): jnp.einsum('sj,jdc->sdc', selector, grads[0], preferred_element_type=jnp....  13.2 us
  transfers between devices with their start and end apart: 6, of which 6 were waited for; matrix products, arithmetic and copies ran while one was open for 0% of the time, Pallas kernels for 0%

commit v1 on v0

--- a/solution.py
+++ b/solution.py
@@ -87,7 +87,8 @@
         + column_scale[:, None, :] * summed
     )
     update_half = update_full.astype(jnp.bfloat16)
-    gathered = lax.all_gather(update_half, "dp", axis=1, tiled=True)
+    parts = lax.all_gather(update_half, "dp", axis=0, tiled=False)
+    gathered = jnp.concatenate(parts, axis=1)
     gathered = gathered.reshape(capacity, owner_count, own_rows, columns)
     returned = lax.all_to_all(gathered, "own", split_axis=1, concat_axis=0, tiled=True)
     slot_rows = returned.reshape(owner_count * capacity, own_rows, columns)

time: 448 us -> 434 us (0.969)
  local copies, waits for them, and re-layouts: 33.4 us -> 19.6 us
    reshape x2 -> x1, local copies, waits for them, and re-layouts: 22.4 us -> 3.2 us  [local(): gathered = jnp.concatenate(parts, axis=1)]
where the time goes in v1:
time: 434 us; the launch traced here: 433 us
  waiting for transfers between devices  341 us (79%)
  matrix products  30.5 us (7%)
  local copies, waits for them, and re-layouts  19.6 us (5%)
  between operations  13.9 us (3%)
  starting transfers between devices  13.7 us (3%)
  blocking collectives  10 us (2%)
  other arithmetic  4.87 us (1%)
    all_to_all x1, waiting for transfers between devices, local(): lax.all_to_all(gathered, 'own', split_axis=1, concat_axis=0, tiled=True)  137 us
    reduce_scatter x1, waiting for transfers between devices, local(): lax.psum_scatter(blocked, 'dp', scatter_dimension=1, tiled=True)  64.6 us
    psum x1, waiting for transfers between devices, local(): lax.psum(partial_value.astype(jnp.bfloat16), 'dp').astype(jnp.float32)  52.7 us
    all_gather x1, waiting for transfers between devices, local(): parts = lax.all_gather(update_half, 'dp', axis=0, tiled=False)  45.6 us
    all_to_all x1, waiting for transfers between devices, local(): lax.all_to_all(placed.astype(jnp.bfloat16), 'dp', split_axis=0, concat_ax...  20.9 us
    all_to_all x1, waiting for transfers between devices, local(): lax.all_to_all(pieces.astype(jnp.bfloat16), 'own', split_axis=0, concat_a...  19.8 us
    dot_general x1, matrix products, local(): jnp.einsum('sj,jdc->sdc', selector, grads[0], preferred_element_type=jnp....  13.2 us
    all_gather x1, blocking collectives, local(): adam_full = lax.all_gather(adam_half, 'dp', axis=1, tiled=True)  10 us
  transfers between devices with their start and end apart: 6, of which 6 were waited for; matrix products, arithmetic and copies ran while one was open for 0% of the time, Pallas kernels for 0%

profile of v1, /device:TPU:0, one launch (start us, length us, event | category | flops | bytes accessed | tf_op | source)
XLA Modules:
  0.0 433.4 jit_solution(5833051217029918127)
XLA Ops:
  7.2 0.0 copy-start
  7.2 0.0 reduce-scatter.2.cloned.1.call-start
  7.2 1.0 convert_reduce_fusion
  8.2 0.8 copy-done
  9.1 13.2 %convolution_convert_fusion = bf16[12,2048,128]{2,0,1:T(8,128)(2,1)S(1)} fusion(bf16[6,2048,128]{2,1,0:T(8,128)(2,1)S(1)} %bitcast.62, s32[12]{0:T(128)S(1)} %get-tuple-element.24, s32[12]{0:T(128)S(1)} %get-tuple-element.25, s32[6]{0:T(128)S(1)} %convert_reduce_fusion, s32[6]{0:T(128)} %param.9), kind=kOutput, calls=%fused_computation.2 | convolution fusion | flops 40894680 | bytes 9437328 | tf_op jit(solution)/shard_map/sj,jdc->sdc/dot_general | solution.py:43
  22.3 4.4 %copy.61 = bf16[12,8,256,128]{3,2,0,1:T(8,128)(2,1)} copy(bf16[12,8,256,128]{3,0,2,1:T(8,128)(2,1)S(1)} %bitcast.63) | data formatting | bytes 12582912 | tf_op jit(solution)/shard_map/reshape | solution.py:48
  26.8 0.0 reduce-scatter.2.cloned.1.call-update
  26.8 64.6 %reduce-scatter.2.cloned.1.call-done = bf16[12,1,256,128]{3,2,0,1:T(8,128)(2,1)} async-done(((bf16[12,8,256,128]{3,2,0,1:T(8,128)(2,1)}), bf16[12,1,256,128]{3,2,0,1:T(8,128)(2,1)}) %reduce-scatter.2.cloned.1.call-update) | async-done | bytes 786448 | tf_op jit(solution)/shard_map/reduce_scatter | solution.py:49
  91.4 4.6 %all-to-all-start = ((bf16[4,3,256,128]{3,2,1,0:T(8,128)(2,1)}), bf16[4,3,256,128]{3,2,1,0:T(8,128)(2,1)S(1)}, u32[]{:S(2)}, u32[]{:S(2)}) async-start(bf16[4,3,256,128]{3,2,1,0:T(8,128)(2,1)} %bitcast.67), calls=%async_computation.1 | async-start | bytes 1572864 | tf_op jit(solution)/shard_map/all_to_all | solution.py:51
  96.0 0.1 mul.82
  96.1 19.8 %all-to-all-done = bf16[4,3,256,128]{3,2,1,0:T(8,128)(2,1)S(1)} async-done(((bf16[4,3,256,128]{3,2,1,0:T(8,128)(2,1)}), bf16[4,3,256,128]{3,2,1,0:T(8,128)(2,1)S(1)}, u32[]{:S(2)}, u32[]{:S(2)}) %all-to-all-start) | async-done | bytes 786464 | tf_op jit(solution)/shard_map/all_to_all | solution.py:51
  116.0 0.1 convert_element_type.58
  116.1 1.6 fusion.7
  117.7 3.6 all-to-all-start.1
  121.3 0.0 all-reduce.2.cloned.1.call-start
  121.3 20.9 %all-to-all-done.1 = bf16[8,3,256,128]{3,2,1,0:T(8,128)(2,1)S(1)} async-done(((bf16[8,3,256,128]{3,2,1,0:T(8,128)(2,1)}), bf16[8,3,256,128]{3,2,1,0:T(8,128)(2,1)S(1)}, u32[]{:S(2)}, u32[]{:S(2)}) %all-to-all-start.1) | async-done | bytes 1572896 | tf_op jit(solution)/shard_map/all_to_all | solution.py:58
  142.2 0.1 convert_bitcast_fusion
  142.4 0.8 copy.62
  143.2 0.8 reshape.73
  144.0 0.0 copy-start.3
  144.0 0.0 copy-start.4
  144.0 4.7 %fusion.19 = bf16[3,1024,128]{1,2,0:T(8,128)(2,1)} fusion(bf16[1,3,1024,1024]{3,2,1,0:T(8,128)(2,1)} %param.6, f32[3,1024,128]{1,2,0:T(8,128)S(1)} %reshape.73), kind=kOutput, calls=%fused_computation.20 | convolution fusion | flops 806092800 | bytes 8650752 | tf_op jit(solution)/shard_map/kdr,kdc->krc/dot_general | solution.py:67
  148.8 0.0 all-reduce.2.cloned.1.call-update
  148.8 0.0 all-gather.3.cloned.1.call-start
  148.8 0.0 copy-done.3
  148.8 0.1 copy.59
  149.0 0.0 copy-done.4
  149.0 0.1 copy.63
  149.1 52.7 %all-reduce.2.cloned.1.call-done = bf16[3,1024,128]{1,2,0:T(8,128)(2,1)} async-done(((bf16[3,1024,128]{1,2,0:T(8,128)(2,1)}), bf16[3,1024,128]{1,2,0:T(8,128)(2,1)}) %all-reduce.2.cloned.1.call-update) | async-done | bytes 786448 | tf_op jit(solution)/shard_map/psum | solution.py:72
  201.8 1.4 convert_element_type.64
  203.2 0.2 fusion.28
  203.4 10.0 %all_gather.9 = bf16[3,1024,128]{1,2,0:T(8,128)(2,1)S(1)} all-gather(bf16[3,128,128]{1,2,0:T(8,128)(2,1)S(1)} %get-tuple-element.22), channel_id=1, replica_groups=mesh['dp'=8,'own'=4] {'dp'}, dimensions={1}, use_global_device_ids=true | all-gather | bytes 884736 | tf_op jit(solution)/shard_map/all_gather | solution.py:76
  213.4 0.2 fusion.11
  213.6 0.0 copy-done.2
  213.6 0.2 multiply_reduce_fusion
  213.9 5.9 %fusion.13 = bf16[3,1024,128]{1,2,0:T(8,128)(2,1)} fusion(f32[3,1024,128]{1,2,0:T(8,128)S(1)} %reshape.73, bf16[1,3,1024,1024]{3,2,1,0:T(8,128)(2,1)} %param.6, bf16[3,1024,128]{1,2,0:T(8,128)(2,1)S(1)} %all_gather.9, f32[3,128]{1,0:T(4,128)S(1)} %add_divide_fusion, bf16[3,1024,128]{1,2,0:T(8,128)(2,1)S(1)} %copy-done.2), kind=kOutput, calls=%fused_computation.17 | convolution fusion | flops 808452096 | bytes 10225152 | tf_op jit(solution)/shard_map/kdr,krc->kdc/dot_general | solution.py:86
  219.8 2.3 copy.64
  222.1 0.0 all-gather.3.cloned.1.call-update
  222.1 45.6 %all-gather.3.cloned.1.call-done = bf16[24,1024,128]{2,1,0:T(8,128)(2,1)} async-done(((bf16[3,1024,128]{2,1,0:T(8,128)(2,1)}), bf16[24,1024,128]{2,1,0:T(8,128)(2,1)}) %all-gather.3.cloned.1.call-update) | async-done | bytes 6291472 | tf_op jit(solution)/shard_map/all_gather | solution.py:90
  267.7 3.2 copy.65
  270.9 3.1 copy.66
  274.0 5.4 %all-to-all-start.2 = ((bf16[3,4,2048,128]{3,2,0,1:T(8,128)(2,1)}), bf16[3,4,2048,128]{3,2,0,1:T(8,128)(2,1)}, u32[]{:S(2)}, u32[]{:S(2)}) async-start(bf16[3,4,2048,128]{3,2,0,1:T(8,128)(2,1)} %copy.66), calls=%async_computation.3 | async-start | bytes 12582912 | tf_op jit(solution)/shard_map/all_to_all | solution.py:93
  279.3 0.8 copy.69
  280.1 0.8 copy.70
  280.9 137.2 %all-to-all-done.2 = bf16[3,4,2048,128]{3,2,0,1:T(8,128)(2,1)} async-done(((bf16[3,4,2048,128]{3,2,0,1:T(8,128)(2,1)}), bf16[3,4,2048,128]{3,2,0,1:T(8,128)(2,1)}, u32[]{:S(2)}, u32[]{:S(2)}) %all-to-all-start.2) | async-done | bytes 6291488 | tf_op jit(solution)/shard_map/all_to_all | solution.py:93
  418.2 0.0 copy-done.5
  418.2 6.7 %fusion.8 = bf16[6,2048,128]{2,0,1:T(8,128)(2,1)S(1)} fusion(bf16[12,2048,128]{2,1,0:T(8,128)(2,1)} %bitcast.18, s32[12]{0:T(128)S(1)} %get-tuple-element.24, s32[12]{0:T(128)S(1)} %get-tuple-element.25, s32[6]{0:T(128)S(1)} %convert_reduce_fusion, s32[6]{0:T(128)S(1)} %copy-done.5), kind=kOutput, calls=%fused_computation.10 | convolution fusion | flops 39321816 | bytes 9437328 | tf_op jit(solution)/shard_map/sj,sdc->jdc/dot_general | solution.py:95
  424.8 2.1 copy.68
  (8 shorter events, 0.0 us)
Async XLA Ops:
  7.2 1.9 copy-start
  7.2 84.2 %reduce-scatter.2.cloned.1.call-start = ((), (), s32[]{:S(2)}) async-start(), calls=%async_computation.4 | async-start | bytes 7077888 | tf_op jit(solution)/shard_map/reduce_scatter | solution.py:49
  91.4 24.6 %all-to-all-start = ((bf16[4,3,256,128]{3,2,1,0:T(8,128)(2,1)}), bf16[4,3,256,128]{3,2,1,0:T(8,128)(2,1)S(1)}, u32[]{:S(2)}, u32[]{:S(2)}) async-start(bf16[4,3,256,128]{3,2,1,0:T(8,128)(2,1)} %bitcast.67), calls=%async_computation.1 | async-start | bytes 1572864 | tf_op jit(solution)/shard_map/all_to_all | solution.py:51
  117.7 24.5 %all-to-all-start.1 = ((bf16[8,3,256,128]{3,2,1,0:T(8,128)(2,1)}), bf16[8,3,256,128]{3,2,1,0:T(8,128)(2,1)S(1)}, u32[]{:S(2)}, u32[]{:S(2)}) async-start(bf16[8,3,256,128]{3,2,1,0:T(8,128)(2,1)} %fusion.7), calls=%async_computation.2 | async-start | bytes 3145728 | tf_op jit(solution)/shard_map/all_to_all | solution.py:58
  121.3 80.5 %all-reduce.2.cloned.1.call-start = ((), (), s32[]{:S(2)}) async-start(), calls=%async_computation.5 | async-start | bytes 1572864 | tf_op jit(solution)/shard_map/psum | solution.py:72
  144.0 4.8 %copy-start.3 = (f32[1,3,128,128]{3,2,1,0:T(8,128)S(1)}, f32[1,3,128,128]{3,2,1,0:T(8,128)}, u32[]{:S(2)}) copy-start(f32[1,3,128,128]{3,2,1,0:T(8,128)} %param.7) | copy-start | bytes 589828
  144.0 4.9 %copy-start.4 = (f32[1,3,128,128]{3,2,1,0:T(8,128)S(1)}, f32[1,3,128,128]{3,2,1,0:T(8,128)}, u32[]{:S(2)}) copy-start(f32[1,3,128,128]{3,2,1,0:T(8,128)} %param.8) | copy-start | bytes 589828
  148.8 118.9 %all-gather.3.cloned.1.call-start = ((), (), s32[]{:S(2)}) async-start(), calls=%async_computation.6 | async-start | bytes 7077888 | tf_op jit(solution)/shard_map/all_gather | solution.py:90
  201.8 11.8 %copy-start.2 = (bf16[3,1024,128]{1,2,0:T(8,128)(2,1)S(1)}, bf16[3,1024,128]{1,2,0:T(8,128)(2,1)}, u32[]{:S(2)}) copy-start(bf16[3,1024,128]{1,2,0:T(8,128)(2,1)} %all-reduce.2.cloned.1.call-done) | copy-start | bytes 2359300
  274.0 144.2 %copy-start.5 = (s32[6]{0:T(128)S(1)}, s32[6]{0:T(128)}, u32[]{:S(2)}) copy-start(s32[6]{0:T(128)} %param.9) | copy-start | bytes 76
  274.0 144.2 %all-to-all-start.2 = ((bf16[3,4,2048,128]{3,2,0,1:T(8,128)(2,1)}), bf16[3,4,2048,128]{3,2,0,1:T(8,128)(2,1)}, u32[]{:S(2)}, u32[]{:S(2)}) async-start(bf16[3,4,2048,128]{3,2,0,1:T(8,128)(2,1)} %copy.66), calls=%async_computation.3 | async-start | bytes 12582912 | tf_op jit(solution)/shard_map/all_to_all | solution.py:93
  418.2 8.8 %copy-start.1 = (bf16[1,6,2048,128]{3,2,1,0:T(8,128)(2,1)S(1)}, bf16[1,6,2048,128]{3,2,1,0:T(8,128)(2,1)}, u32[]{:S(2)}) copy-start(bf16[1,6,2048,128]{3,2,1,0:T(8,128)(2,1)} %param.5) | copy-start | bytes 9437188
Sparse Core Ops, SparseCore 0:
  26.9 64.4 reduce-scatter.1
  148.9 52.8 all-reduce.1
  222.2 45.3 all-gather.2
